TPU v7x, 512 devices: a whole 4x4x16 slice. The times are simulated.
512 devices in a mesh: pb: 128 (over y, z, core), slab: 4 (over x).
Axes of the slice: x: 4, y: 4, z: 16, core: 2. Of those that a mesh axis runs over, the one named last changes fastest.
Arguments:
- query_feats: bfloat16 [128, 128, 9, 256], P('pb', 'slab'), may hold values from -1.5 to 1.5
- frame_store: bfloat16 [512, 128, 9, 256], P(None, 'pb'), may hold values from -1.5 to 1.5
- candidates: int32 [128, 4], replicated, may hold values from 0 to 511
- query_length: int32 [128], P('pb'), may hold values from 16 to 128, as said below
- clip_length: int32 [512], replicated, may hold values from 16 to 128, as said below
- kernel_one: float32 [3, 3, 1, 32], replicated, may hold values from -2 to 2
- bias_one: float32 [32], replicated, may hold values from -0.2 to 0.2
- kernel_two: float32 [3, 3, 32, 64], replicated, may hold values from -0.375 to 0.375
- bias_two: float32 [64], replicated, may hold values from -0.2 to 0.2
- kernel_three: float32 [3, 3, 64, 128], replicated, may hold values from -0.25 to 0.25
- bias_three: float32 [128], replicated, may hold values from -0.2 to 0.2
- kernel_four: float32 [1, 1, 128, 1], replicated, may hold values from -0.5 to 0.5
- bias_four: float32 [1], replicated, may hold values from -1.75 to 1.75
Outputs:
- scores: float32 [128, 4], P('pb')
Inputs may be any that keep to these rules, and one draw needn't show every extreme that they name: `query_length`: some query has exactly 128 valid frames and some exactly 16. `clip_length`: some candidate clip has exactly 128 valid frames and some exactly 16.
All inputs are finite; a program needn't handle non-finite values.
Results may differ from a plain program's by a relative error of at most 0.0003.
Values may be sent and summed in bfloat16 or wider, within the bound.
A program may use at most 128 MiB of HBM per device.

v0:
```python
import functools

import jax
import jax.numpy as jnp
from jax import lax
from jax.experimental import pallas as pl
from jax.experimental.pallas import tpu as pltpu
from jax.sharding import PartitionSpec as P

NY, NZ, NC, NX = 4, 16, 2, 4
NSLOT = NY * NC
NCHUNK = 3
SPER = 3
MESH = pl.DeviceIdType.MESH
BF = jnp.bfloat16
F32 = jnp.float32
Z_ORDER = (8, 7, 9, 6, 10, 5, 11, 4, 12, 3, 13, 2, 14, 1, 15)


def iota(shape, dim):
    return lax.broadcasted_iota(jnp.int32, shape, dim)


def dot(a, b):
    return lax.dot_general(a, b, (((1,), (0,)), ((), ())), preferred_element_type=F32)


def dot_t(a, b):
    return lax.dot_general(a, b, (((1,), (1,)), ((), ())), preferred_element_type=F32)


def hot(mask):
    return jnp.where(mask, 1.0, 0.0).astype(BF)


def halves(x):
    hi = x.astype(BF)
    lo = (x - hi.astype(F32)).astype(BF)
    return hi, lo


def prepare(k1, b1, k2, b2, k3, b3, k4, sq, w1, w2, w3, b2c, k4c, p1f, p1b, p3h, p3l):
    sq[...] = jnp.zeros_like(sq)
    for tap in range(9):
        sq[tap : tap + 1, 0:32] = k1[tap]
    sq[9:10, 0:32] = b1[...]
    hi, lo = halves(jnp.transpose(sq[...])[0:32])
    t = iota((128, 256), 0)
    k = iota((128, 256), 1)
    ti = jnp.where(t >= 3, 1, 0) + jnp.where(t >= 6, 1, 0)
    tj = t - 3 * ti
    for phase in range(16):
        row = 2 * (phase >> 3) + ((phase >> 1) & 1)
        col = 2 * ((phase >> 2) & 1) + (phase & 1)
        at = jnp.where(t == 9, 36, (row + ti) * 6 + col + tj)
        at = jnp.where(t > 9, -1000, at)
        both = hot((k == at) | (k == at + 48))
        last = hot(k == at + 96)
        w1[phase * 32 : phase * 32 + 32, :] = (dot(hi, both) + dot(lo, last)).astype(BF)
    w2[...] = jnp.zeros_like(w2)
    for ti in range(3):
        sq[...] = jnp.zeros_like(sq)
        sq[0:96, 0:64] = k2[ti * 96 : ti * 96 + 96, :]
        block = jnp.transpose(sq[...])[0:64]
        for a in range(2):
            for b in range(2):
                hi, lo = halves(block if b == 0 else pltpu.roll(block, 32, 1))
                lanes = slice((a + ti) * 128, (a + ti) * 128 + 128)
                row = (a * 2 + b) * 64
                w2[row : row + 64, lanes] = hi
                w2[256 + row : 256 + row + 64, lanes] = lo
    sq[...] = jnp.zeros_like(sq)
    sq[:, 0:64] = jnp.broadcast_to(b2[...], (128, 64))
    b2c[...] = jnp.transpose(sq[...])[0:64]
    for part in range(5):
        if part < 4:
            block = k3[part * 128 : part * 128 + 128, :]
        else:
            sq[...] = jnp.zeros_like(sq)
            sq[0:64, :] = k3[512:576, :]
            sq[64:65, :] = b3[...]
            block = sq[...]
        hi, lo = halves(jnp.transpose(block))
        w3[0:128, part * 128 : part * 128 + 128] = hi
        w3[128:256, part * 128 : part * 128 + 128] = lo
    k4c[...] = jnp.transpose(jnp.broadcast_to(k4[...], (128, 128)))
    p1b[144:256, :] = jnp.zeros((112, 1024), BF)
    ones = jnp.where(iota((16, 128), 0) == 4, 1.0, 0.0)
    for u in range(8):
        p1f[u * 48 + 32 : u * 48 + 48, :] = ones
    p3h[576:640, :] = hot(iota((64, 1024), 0) == 0)
    p3l[576:640, :] = jnp.zeros((64, 1024), BF)


def gram_chunk(chunk, qbuf, x, best):
    blocks = []
    for s in range(SPER):
        for e in range(2):
            blocks.append(x[chunk, :, s, e].reshape(64, 256))
    right = jnp.concatenate(blocks, axis=0)
    for r in range(9):
        g = dot_t(qbuf[:, r].reshape(128, 256), right)
        m = jnp.maximum(jnp.maximum(g[:, 0:128], g[:, 128:256]), g[:, 256:384])
        best[r] = m if chunk == 0 else jnp.maximum(best[r], m)


def refine(best, qlen, clen, b4, w1, w2, w3, b2c, k4c, p1f, p1b, p2h, p2l, p3h, p3l):
    lane = iota((8, 128), 1)
    sub = iota((8, 128), 0)
    grp = lane >> 5
    col = lane & 31
    total = best[0]
    for r in range(1, 9):
        total = total + best[r]
    total = total * (1.0 / 9.0)
    keep_col = (4 * col + grp) < clen
    sim = []
    for g in range(4):
        line = []
        for sg in range(4):
            at = (g * 4 + sg) * 8
            keep = keep_col & ((32 * g + 4 * sub + sg) < qlen)
            line.append(jnp.where(keep, total[at : at + 8], 0.0))
        sim.append(line)

    def up(x, nrow):
        y = pltpu.roll(x, 1, 0)
        z = jnp.where(grp == 0, 0.0, pltpu.roll(y, 32, 1))
        return jnp.where(sub == 0, z, y)

    def down(x, nrow):
        y = pltpu.roll(x, 7, 0)
        z = jnp.where(grp == 3, 0.0, pltpu.roll(y, 96, 1))
        return jnp.where(sub == 7, z, y)

    base = {}
    for sg in range(4):
        for rho in range(4):
            out = None
            for g in range(4):
                shift = ((g - rho) * 32) % 128
                piece = sim[g][sg] if shift == 0 else pltpu.roll(sim[g][sg], shift, 1)
                out = piece if out is None else jnp.where(grp == g, piece, out)
            base[sg, rho] = out
    rows = {}
    for rho in range(4):
        for sg in range(4):
            rows[sg, rho] = base[sg, rho]
        rows[-1, rho] = up(base[3, rho], 8)
        rows[4, rho] = down(base[0, rho], 8)
    for d in range(-1, 5):
        for e in range(-1, 5):
            if e == -1:
                v = jnp.where(col == 0, 0.0, pltpu.roll(rows[d, 3], 1, 1))
            elif e == 4:
                v = jnp.where(col == 31, 0.0, pltpu.roll(rows[d, 0], 127, 1))
            else:
                v = rows[d, e]
            p1f[pl.ds((d + 1) * 6 + e + 1, 8, stride=48), :] = v
    for u in range(8):
        hi, lo = halves(p1f[u * 48 : u * 48 + 48, :])
        lanes = slice(u * 128, u * 128 + 128)
        p1b[0:48, lanes] = hi
        p1b[48:96, lanes] = lo
        p1b[96:144, lanes] = hi

    def tall(x, n):
        return jnp.broadcast_to(x[0:1], (n, 128))

    grp32, col32 = tall(grp, 32), tall(col, 32)
    grp64, col64 = tall(grp, 64), tall(col, 64)

    def put(high, low, at, n, u, value):
        hi, lo = halves(value)
        high[at : at + n, u * 128 : u * 128 + 128] = hi
        low[at : at + n, u * 128 : u * 128 + 128] = lo
        return hi, lo

    def put_above(high, low, at, n, u, value, pair, groups):
        if u < 7:
            high[at : at + n, u * 128 + 128 : u * 128 + 256] = pair[0]
            low[at : at + n, u * 128 + 128 : u * 128 + 256] = pair[1]
        else:
            put(high, low, at, n, 0, jnp.where(groups == 0, 0.0, pltpu.roll(value, 32, 1)))

    def put_below(high, low, at, n, u, value, pair, groups):
        if u > 0:
            high[at : at + n, u * 128 - 128 : u * 128] = pair[0]
            low[at : at + n, u * 128 - 128 : u * 128] = pair[1]
        else:
            put(high, low, at, n, 7, jnp.where(groups == 3, 0.0, pltpu.roll(value, 96, 1)))

    for tile in range(4):
        o1 = dot(w1[...], p1b[:, tile * 256 : tile * 256 + 256])
        for ab in range(4):
            a, b = ab >> 1, ab & 1
            part = o1[ab * 128 : ab * 128 + 128]
            m = jnp.maximum(
                jnp.maximum(part[0:32], part[32:64]), jnp.maximum(part[64:96], part[96:128])
            )
            m = jnp.maximum(m, 0.0)
            for half in range(2):
                u = tile * 2 + half
                v = m[:, half * 128 : half * 128 + 128]
                if b == 1:
                    moved = jnp.where(col32 == 0, 0.0, pltpu.roll(v, 1, 1))
                    variants = ((2, v), (0, moved))
                else:
                    moved = jnp.where(col32 == 31, 0.0, pltpu.roll(v, 127, 1))
                    variants = ((1, v), (3, moved))
                for e, w in variants:
                    if a == 0:
                        pair = put(p2h, p2l, (4 + e) * 32, 32, u, w)
                        put_below(p2h, p2l, (12 + e) * 32, 32, u, w, pair, grp32)
                    else:
                        pair = put(p2h, p2l, (8 + e) * 32, 32, u, w)
                        put_above(p2h, p2l, e * 32, 32, u, w, pair, grp32)
    for tile in range(4):
        lanes = slice(tile * 256, tile * 256 + 256)
        first = dot(w2[...], p2h[:, lanes])
        o2 = first[0:256] + (first[256:512] + dot(w2[0:256, :], p2l[:, lanes]))
        m = jnp.maximum(
            jnp.maximum(o2[0:64], o2[64:128]), jnp.maximum(o2[128:192], o2[192:256])
        )
        for half in range(2):
            u = tile * 2 + half
            v = jnp.maximum(m[:, half * 128 : half * 128 + 128] + b2c[...], 0.0)
            left = jnp.where(col64 == 0, 0.0, pltpu.roll(v, 1, 1))
            right = jnp.where(col64 == 31, 0.0, pltpu.roll(v, 127, 1))
            for dj, w in ((0, left), (1, v), (2, right)):
                pair = put(p3h, p3l, (3 + dj) * 64, 64, u, w)
                put_above(p3h, p3l, dj * 64, 64, u, w, pair, grp64)
                put_below(p3h, p3l, (6 + dj) * 64, 64, u, w, pair, grp64)
    final = []
    for tile in range(4):
        lanes = slice(tile * 256, tile * 256 + 256)
        first = dot(w3[...], p3h[:, lanes])
        o3 = first[0:128] + (first[128:256] + dot(w3[0:128, :], p3l[:, lanes]))
        o3 = jnp.maximum(o3, 0.0)
        for half in range(2):
            v = o3[:, half * 128 : half * 128 + 128] * k4c[...]
            final.append(jnp.sum(v, axis=0, keepdims=True))
    field = jnp.clip(jnp.concatenate(final, axis=0) + b4, -1.0, 1.0)
    m = jnp.where(4 * col < clen, field, -2.0)
    for step in (1, 2, 4, 8, 16):
        m = jnp.maximum(m, pltpu.roll(m, 128 - step, 1))
    counted = (col == 0) & (4 * (grp * 8 + sub) < qlen)
    score = jnp.sum(jnp.where(counted, m, 0.0), keepdims=True)
    number = ((jnp.full((8, 128), qlen, jnp.int32) + 3) >> 2).astype(F32)
    return jnp.broadcast_to(score, (8, 128)) / number


def kernel(
    q_ref, f_ref, cand_v, cand_s, qlen_ref, clen_ref,
    k1, b1, k2, b2, k3, b3, k4, b4,
    out_ref,
    frames, outgoing, landed, mid, x, qbuf, best, sq, w1, w2, w3, b2c, k4c,
    p1f, p1b, p2h, p2l, p3h, p3l, scores,
    f_sem, a_send, a_recv, b_send, b_recv, q_send, q_recv, s_send, s_recv,
):
    pb = lax.axis_index("pb")
    slab = lax.axis_index("slab")
    my_y = lax.div(pb, NZ * NC)
    my_z = lax.rem(lax.div(pb, NC), NZ)
    my_c = lax.rem(pb, NC)
    my_slot = my_c * NY + my_y

    def z_peer(step):
        z = lax.rem(my_z + step, NZ)
        return z, ((my_y * NZ + z) * NC + my_c, slab)

    def slot_peer(step):
        slot = lax.rem(my_slot + step, NSLOT)
        y, c = lax.rem(slot, NY), lax.div(slot, NY)
        return slot, ((y * NZ + my_z) * NC + c, slab)

    def x_peer(step):
        other = lax.rem(slab + step, NX)
        return other, (pb, other)

    barrier = pltpu.get_barrier_semaphore()
    for step in Z_ORDER:
        pl.semaphore_signal(barrier, inc=1, device_id=z_peer(step)[1], device_id_type=MESH)
    for step in range(1, NSLOT):
        pl.semaphore_signal(barrier, inc=1, device_id=slot_peer(step)[1], device_id_type=MESH)
    for step in range(1, NX):
        pl.semaphore_signal(barrier, inc=1, device_id=x_peer(step)[1], device_id_type=MESH)

    def fetch(chunk):
        return pltpu.make_async_copy(
            f_ref.at[pl.ds(chunk * SPER, SPER)], frames.at[chunk], f_sem.at[chunk]
        )

    for chunk in range(NCHUNK):
        fetch(chunk).start()

    n = iota((128, 128), 0)
    asks = ((n & 3) * NZ + (n >> 3)) * NC + ((n >> 2) & 1)
    order = hot(iota((128, 128), 1) == asks)
    wanted = jnp.broadcast_to(cand_v[pl.ds(slab, 1), :], (512, 128))
    select = dot_t(order, hot(iota((512, 128), 0) == wanted)).astype(BF)

    def gather(chunk):
        for s in range(SPER):
            rows = dot(select, frames[chunk, s])
            outgoing[chunk, s] = rows.reshape(NZ, NSLOT, 256).astype(BF)

    qi = iota((32, 32), 0)
    pick = hot(iota((32, 32), 1) == 4 * (qi & 7) + (qi >> 3))
    for r in range(9):
        qbuf[slab, r] = dot(pick, q_ref[r]).reshape(4, 8, 256).astype(BF)
    fetch(0).wait()
    gather(0)

    def send_a(chunk, step):
        z, device = z_peer(step)
        return pltpu.make_async_remote_copy(
            src_ref=outgoing.at[chunk, :, z],
            dst_ref=landed.at[chunk, my_z],
            send_sem=a_send.at[chunk, step],
            recv_sem=a_recv.at[chunk, my_z],
            device_id=device,
            device_id_type=MESH,
        )

    def recv_a(chunk, step):
        z, device = z_peer(step)
        return pltpu.make_async_remote_copy(
            src_ref=outgoing.at[chunk, :, z],
            dst_ref=landed.at[chunk, z],
            send_sem=a_send.at[chunk, step],
            recv_sem=a_recv.at[chunk, z],
            device_id=device,
            device_id_type=MESH,
        )

    def send_b(chunk, step):
        slot, device = slot_peer(step)
        return pltpu.make_async_remote_copy(
            src_ref=mid.at[chunk, slot],
            dst_ref=x.at[chunk, my_slot],
            send_sem=b_send.at[chunk, step],
            recv_sem=b_recv.at[chunk, my_slot],
            device_id=device,
            device_id_type=MESH,
        )

    def recv_b(chunk, step):
        slot, device = slot_peer(step)
        return pltpu.make_async_remote_copy(
            src_ref=mid.at[chunk, slot],
            dst_ref=x.at[chunk, slot],
            send_sem=b_send.at[chunk, step],
            recv_sem=b_recv.at[chunk, slot],
            device_id=device,
            device_id_type=MESH,
        )

    def x_copy(buffer, send, recv, step, arriving):
        other, device = x_peer(step)
        place = other if arriving else slab
        return pltpu.make_async_remote_copy(
            src_ref=buffer.at[slab],
            dst_ref=buffer.at[place],
            send_sem=send.at[step],
            recv_sem=recv.at[place],
            device_id=device,
            device_id_type=MESH,
        )

    pl.semaphore_wait(barrier, NZ - 1 + NSLOT - 1 + NX - 1)
    for step in Z_ORDER:
        send_a(0, step).start()
    for step in range(1, NX):
        x_copy(qbuf, q_send, q_recv, step, False).start()
    for chunk in range(1, NCHUNK):
        fetch(chunk).wait()
        gather(chunk)
        for step in Z_ORDER:
            send_a(chunk, step).start()

    prepare(k1, b1, k2, b2, k3, b3, k4, sq, w1, w2, w3, b2c, k4c, p1f, p1b, p3h, p3l)

    m = iota((128, 128), 0)
    source = (2 * (m & 7) + ((m >> 3) & 1)) * NSLOT + (m >> 4)
    shuffle = hot(iota((128, 128), 1) == source)

    def finish(chunk):
        for step in range(1, NSLOT):
            recv_b(chunk, step).wait_recv()
        gram_chunk(chunk, qbuf, x, best)

    for chunk in range(NCHUNK):
        for step in Z_ORDER:
            recv_a(chunk, step).wait_recv()
        for s in range(SPER):
            landed[chunk, my_z, s] = outgoing[chunk, s, my_z]
        for s in range(SPER):
            rows = dot(shuffle, landed[chunk, :, s].reshape(128, 256))
            mid[chunk, :, s] = rows.reshape(NSLOT, 2, 8, 256).astype(BF)
        for step in range(1, NSLOT):
            send_b(chunk, step).start()
        x[chunk, my_slot] = mid[chunk, my_slot]
        if chunk == 0:
            for step in range(1, NX):
                x_copy(qbuf, q_send, q_recv, step, True).wait_recv()
        else:
            finish(chunk - 1)
    finish(NCHUNK - 1)

    qlen = qlen_ref[0]
    clen = clen_ref[cand_s[slab, pb]]
    scores[slab] = refine(
        best, qlen, clen, b4[0], w1, w2, w3, b2c, k4c, p1f, p1b, p2h, p2l, p3h, p3l
    )
    for step in range(1, NX):
        x_copy(scores, s_send, s_recv, step, False).start()
    for chunk in range(NCHUNK):
        for step in Z_ORDER:
            send_a(chunk, step).wait_send()
        for step in range(1, NSLOT):
            send_b(chunk, step).wait_send()
    for step in range(1, NX):
        x_copy(qbuf, q_send, q_recv, step, False).wait_send()
    for step in range(1, NX):
        x_copy(scores, s_send, s_recv, step, True).wait_recv()
    for step in range(1, NX):
        x_copy(scores, s_send, s_recv, step, False).wait_send()
    where = iota((1, 128), 1)
    line = scores[0, 0:1]
    for other in range(1, NX):
        line = jnp.where(where == other, scores[other, 0:1], line)
    out_ref[...] = line[:, 0:4]


def compute_scratch():
    return [
        pltpu.VMEM((9, 128, 128), F32),
        pltpu.VMEM((128, 128), F32),
        pltpu.VMEM((512, 256), BF),
        pltpu.VMEM((512, 512), BF),
        pltpu.VMEM((256, 640), BF),
        pltpu.VMEM((64, 128), F32),
        pltpu.VMEM((128, 128), F32),
        pltpu.VMEM((384, 128), F32),
        pltpu.VMEM((256, 1024), BF),
        pltpu.VMEM((512, 1024), BF),
        pltpu.VMEM((512, 1024), BF),
        pltpu.VMEM((640, 1024), BF),
        pltpu.VMEM((640, 1024), BF),
    ]


def per_device(
    query_feats, frame_store, candidates, query_length, clip_length,
    kernel_one, bias_one, kernel_two, bias_two, kernel_three, bias_three, kernel_four, bias_four,
):
    vmem = pl.BlockSpec(memory_space=pltpu.VMEM)
    smem = pl.BlockSpec(memory_space=pltpu.SMEM)
    dma = pltpu.SemaphoreType.DMA
    pairs = candidates.T
    return pl.pallas_call(
        kernel,
        out_shape=jax.ShapeDtypeStruct((1, 4), F32),
        in_specs=[vmem, pl.BlockSpec(memory_space=pl.ANY), vmem, smem, smem, smem]
        + [vmem] * 7
        + [smem],
        out_specs=vmem,
        scratch_shapes=[
            pltpu.VMEM((NCHUNK, SPER, 512, 256), BF),
            pltpu.VMEM((NCHUNK, SPER, NZ, NSLOT, 256), BF),
            pltpu.VMEM((NCHUNK, NZ, SPER, NSLOT, 256), BF),
            pltpu.VMEM((NCHUNK, NSLOT, SPER, 2, 8, 256), BF),
            pltpu.VMEM((NCHUNK, NSLOT, SPER, 2, 8, 256), BF),
            pltpu.VMEM((NX, 9, 4, 8, 256), BF),
        ]
        + compute_scratch()
        + [
            pltpu.VMEM((NX, 8, 128), F32),
            dma((NCHUNK,)),
            dma((NCHUNK, NZ)),
            dma((NCHUNK, NZ)),
            dma((NCHUNK, NSLOT)),
            dma((NCHUNK, NSLOT)),
            dma((NX,)),
            dma((NX,)),
            dma((NX,)),
            dma((NX,)),
        ],
        compiler_params=pltpu.CompilerParams(collective_id=0, has_side_effects=True),
        name="score_pairs",
    )(
        query_feats[0].transpose(1, 0, 2),
        frame_store[:, 0].transpose(1, 0, 2),
        pairs,
        pairs,
        query_length,
        clip_length,
        kernel_one.reshape(9, 1, 32),
        bias_one.reshape(1, 32),
        kernel_two.reshape(288, 64),
        bias_two.reshape(1, 64),
        kernel_three.reshape(576, 128),
        bias_three.reshape(1, 128),
        kernel_four.reshape(1, 128),
        bias_four,
    )


def solution(mesh):
    placed = (
        P("pb", "slab", None, None),
        P(None, "pb", None, None),
        P(), P("pb"), P(), P(), P(), P(), P(), P(), P(), P(), P(),
    )
    return jax.shard_map(
        per_device, mesh=mesh, in_specs=placed, out_specs=P("pb", None), check_vma=False
    )
```

profile of v0, /device:TPU:1, one launch (start us, length us, event | category | flops | bytes accessed | tf_op | source)
XLA Modules:
  0.0 61.2 jit_solution(9639069599554165944)
XLA Ops:
  1.3 58.7 %score_pairs.1 = f32[1,4]{1,0:T(1,128)} custom-call(bf16[9,32,256]{2,1,0:T(8,128)(2,1)} %bitcast.16, bf16[9,512,256]{2,1,0:T(8,128)(2,1)} %bitcast.14, s32[4,128]{1,0:T(4,128)} %bitcast.18, s32[4,128]{1,0:T(4,128)} %bitcast.19, s32[1]{0:T(128)S(6)} %copy.15.qlen_ref, s32[512]{0:T(512)} %clen_ref.1, f32[9,1,32]{2,1,0:T(1,128)} %bitcast.20, f32[1,32]{1,0:T(1,128)} %bitcast.21, ...), custom_call_target="tpu_custom_call" | custom-call | tf_op jit(solution)/shard_map/score_pairs/pallas_call | solution.py:462
  60.0 1.2 %copy.17 = f32[1,4]{1,0:T(1,128)} copy(f32[1,4]{1,0:T(1,128)} %score_pairs.1) | data formatting | bytes 32
where the time goes:
time: 61.4 us; the launch traced here: 61.2 us
  Pallas kernels  58.7 us (96%)
  between operations  1.3 us (2%)
  local copies, waits for them, and re-layouts  1.19 us (2%)
    pallas_call x1, Pallas kernels, per_device(): pl.pallas_call(kernel, out_shape=jax.ShapeDtypeStruct((1, 4), F32), in_sp...  58.7 us

commit v1 on v0

--- a/solution.py
+++ b/solution.py
@@ -9,12 +9,13 @@
 
 NY, NZ, NC, NX = 4, 16, 2, 4
 NSLOT = NY * NC
-NCHUNK = 3
-SPER = 3
+CHUNKS = ((0, 2), (2, 5), (5, 9))
+NEAR = 3
 MESH = pl.DeviceIdType.MESH
 BF = jnp.bfloat16
 F32 = jnp.float32
-Z_ORDER = (8, 7, 9, 6, 10, 5, 11, 4, 12, 3, 13, 2, 14, 1, 15)
+Z_NEAR = tuple(step for far in range(1, NEAR + 1) for step in (far, NZ - far))
+Z_FAR = (8,) + tuple(step for far in range(7, NEAR, -1) for step in (far, NZ - far))
 
 
 def iota(shape, dim):
@@ -93,14 +94,17 @@
 
 
 def gram_chunk(chunk, qbuf, x, best):
-    blocks = []
-    for s in range(SPER):
-        for e in range(2):
-            blocks.append(x[chunk, :, s, e].reshape(64, 256))
-    right = jnp.concatenate(blocks, axis=0)
+    first, end = CHUNKS[chunk]
+    p = iota((128, 128), 0)
+    source = (2 * (p & 7) + (p >> 6)) * NSLOT + ((p >> 5) & 1) * NY + ((p >> 3) & 3)
+    place = hot(iota((128, 128), 1) == source)
+    right = [dot(place, x[:, s].reshape(128, 256)).astype(BF) for s in range(first, end)]
+    right = jnp.concatenate(right, axis=0)
     for r in range(9):
         g = dot_t(qbuf[:, r].reshape(128, 256), right)
-        m = jnp.maximum(jnp.maximum(g[:, 0:128], g[:, 128:256]), g[:, 256:384])
+        m = g[:, 0:128]
+        for s in range(1, end - first):
+            m = jnp.maximum(m, g[:, s * 128 : s * 128 + 128])
         best[r] = m if chunk == 0 else jnp.maximum(best[r], m)
 
 
@@ -256,7 +260,7 @@
     out_ref,
     frames, outgoing, landed, mid, x, qbuf, best, sq, w1, w2, w3, b2c, k4c,
     p1f, p1b, p2h, p2l, p3h, p3l, scores,
-    f_sem, a_send, a_recv, b_send, b_recv, q_send, q_recv, s_send, s_recv,
+    f_sem, a_send, a_recv, b_send, b_recv, q_send, q_recv, s_send, s_recv, below, above,
 ):
     pb = lax.axis_index("pb")
     slab = lax.axis_index("slab")
@@ -279,79 +283,56 @@
         return other, (pb, other)
 
     barrier = pltpu.get_barrier_semaphore()
-    for step in Z_ORDER:
-        pl.semaphore_signal(barrier, inc=1, device_id=z_peer(step)[1], device_id_type=MESH)
-    for step in range(1, NSLOT):
-        pl.semaphore_signal(barrier, inc=1, device_id=slot_peer(step)[1], device_id_type=MESH)
-    for step in range(1, NX):
-        pl.semaphore_signal(barrier, inc=1, device_id=x_peer(step)[1], device_id_type=MESH)
+    near = [z_peer(1), z_peer(NZ - 1)]
+    near += [slot_peer(step) for step in range(1, NSLOT)]
+    near += [x_peer(step) for step in range(1, NX)]
+    for _, device in near:
+        pl.semaphore_signal(barrier, inc=1, device_id=device, device_id_type=MESH)
 
     def fetch(chunk):
-        return pltpu.make_async_copy(
-            f_ref.at[pl.ds(chunk * SPER, SPER)], frames.at[chunk], f_sem.at[chunk]
-        )
-
-    for chunk in range(NCHUNK):
+        first, end = CHUNKS[chunk]
+        regions = pl.ds(first, end - first)
+        return pltpu.make_async_copy(f_ref.at[regions], frames.at[regions], f_sem.at[chunk])
+
+    chunks = range(len(CHUNKS))
+    for chunk in chunks:
         fetch(chunk).start()
 
     n = iota((128, 128), 0)
-    asks = ((n & 3) * NZ + (n >> 3)) * NC + ((n >> 2) & 1)
+    asks = (((n >> 4) & 3) * NZ + (n & 15)) * NC + (n >> 6)
     order = hot(iota((128, 128), 1) == asks)
     wanted = jnp.broadcast_to(cand_v[pl.ds(slab, 1), :], (512, 128))
     select = dot_t(order, hot(iota((512, 128), 0) == wanted)).astype(BF)
 
     def gather(chunk):
-        for s in range(SPER):
-            rows = dot(select, frames[chunk, s])
-            outgoing[chunk, s] = rows.reshape(NZ, NSLOT, 256).astype(BF)
-
-    qi = iota((32, 32), 0)
-    pick = hot(iota((32, 32), 1) == 4 * (qi & 7) + (qi >> 3))
-    for r in range(9):
-        qbuf[slab, r] = dot(pick, q_ref[r]).reshape(4, 8, 256).astype(BF)
-    fetch(0).wait()
-    gather(0)
-
-    def send_a(chunk, step):
-        z, device = z_peer(step)
+        fetch(chunk).wait()
+        for s in range(*CHUNKS[chunk]):
+            outgoing[:, s] = dot(select, frames[s]).reshape(NSLOT, NZ, 256).astype(BF)
+
+    def send_b(chunk, step, arriving=False):
+        first, end = CHUNKS[chunk]
+        regions = pl.ds(first, end - first)
+        slot, device = slot_peer(step)
+        place = slot if arriving else my_slot
         return pltpu.make_async_remote_copy(
-            src_ref=outgoing.at[chunk, :, z],
-            dst_ref=landed.at[chunk, my_z],
-            send_sem=a_send.at[chunk, step],
-            recv_sem=a_recv.at[chunk, my_z],
+            src_ref=outgoing.at[slot, regions],
+            dst_ref=landed.at[place, regions],
+            send_sem=b_send.at[chunk, step],
+            recv_sem=b_recv.at[chunk, place],
             device_id=device,
             device_id_type=MESH,
         )
 
-    def recv_a(chunk, step):
+    def send_a(chunk, step, arriving=False):
+        first, end = CHUNKS[chunk]
+        regions = pl.ds(first, end - first)
         z, device = z_peer(step)
+        place = z if arriving else my_z
         return pltpu.make_async_remote_copy(
-            src_ref=outgoing.at[chunk, :, z],
-            dst_ref=landed.at[chunk, z],
+            src_ref=mid.at[z, regions],
+            dst_ref=x.at[place, regions],
             send_sem=a_send.at[chunk, step],
-            recv_sem=a_recv.at[chunk, z],
-            device_id=device,
-            device_id_type=MESH,
-        )
-
-    def send_b(chunk, step):
-        slot, device = slot_peer(step)
-        return pltpu.make_async_remote_copy(
-            src_ref=mid.at[chunk, slot],
-            dst_ref=x.at[chunk, my_slot],
-            send_sem=b_send.at[chunk, step],
-            recv_sem=b_recv.at[chunk, my_slot],
-            device_id=device,
-            device_id_type=MESH,
-        )
-
-    def recv_b(chunk, step):
-        slot, device = slot_peer(step)
-        return pltpu.make_async_remote_copy(
-            src_ref=mid.at[chunk, slot],
-            dst_ref=x.at[chunk, slot],
-            send_sem=b_send.at[chunk, step],
-            recv_sem=b_recv.at[chunk, slot],
+            recv_sem=a_recv.at[chunk, place],
             device_id=device,
             device_id_type=MESH,
         )
@@ -368,45 +349,71 @@
             device_id_type=MESH,
         )
 
-    pl.semaphore_wait(barrier, NZ - 1 + NSLOT - 1 + NX - 1)
-    for step in Z_ORDER:
-        send_a(0, step).start()
+    def tell(k):
+        if k <= 7:
+            pl.semaphore_signal(
+                below.at[k], inc=1, device_id=z_peer(1)[1], device_id_type=MESH
+            )
+        if k <= 6:
+            pl.semaphore_signal(
+                above.at[k], inc=1, device_id=z_peer(NZ - 1)[1], device_id_type=MESH
+            )
+
+    def hear(k):
+        pl.semaphore_wait(below.at[k], 1)
+        if k <= 6:
+            pl.semaphore_wait(above.at[k], 1)
+        tell(k + 1)
+
+    m = iota((128, 128), 0)
+    shuffle = hot(iota((128, 128), 1) == (m & 7) * NZ + (m >> 3))
+
+    def turn(chunk):
+        first, end = CHUNKS[chunk]
+        landed[my_slot, first:end] = outgoing[my_slot, first:end]
+        for step in range(1, NSLOT):
+            send_b(chunk, step, True).wait_recv()
+        for s in range(first, end):
+            rows = dot(shuffle, landed[:, s].reshape(128, 256))
+            mid[:, s] = rows.reshape(NZ, NSLOT, 256).astype(BF)
+
+    gather(0)
+    pl.semaphore_wait(barrier, len(near))
+    tell(1)
+    for step in range(1, NSLOT):
+        send_b(0, step).start()
+    qi = iota((32, 32), 0)
+    pick = hot(iota((32, 32), 1) == 4 * (qi & 7) + (qi >> 3))
+    for r in range(9):
+        qbuf[slab, r] = dot(pick, q_ref[r]).reshape(4, 8, 256).astype(BF)
     for step in range(1, NX):
         x_copy(qbuf, q_send, q_recv, step, False).start()
-    for chunk in range(1, NCHUNK):
-        fetch(chunk).wait()
+    for chunk in chunks[1:]:
         gather(chunk)
-        for step in Z_ORDER:
-            send_a(chunk, step).start()
-
-    prepare(k1, b1, k2, b2, k3, b3, k4, sq, w1, w2, w3, b2c, k4c, p1f, p1b, p3h, p3l)
-
-    m = iota((128, 128), 0)
-    source = (2 * (m & 7) + ((m >> 3) & 1)) * NSLOT + (m >> 4)
-    shuffle = hot(iota((128, 128), 1) == source)
-
-    def finish(chunk):
-        for step in range(1, NSLOT):
-            recv_b(chunk, step).wait_recv()
-        gram_chunk(chunk, qbuf, x, best)
-
-    for chunk in range(NCHUNK):
-        for step in Z_ORDER:
-            recv_a(chunk, step).wait_recv()
-        for s in range(SPER):
-            landed[chunk, my_z, s] = outgoing[chunk, s, my_z]
-        for s in range(SPER):
-            rows = dot(shuffle, landed[chunk, :, s].reshape(128, 256))
-            mid[chunk, :, s] = rows.reshape(NSLOT, 2, 8, 256).astype(BF)
         for step in range(1, NSLOT):
             send_b(chunk, step).start()
-        x[chunk, my_slot] = mid[chunk, my_slot]
-        if chunk == 0:
-            for step in range(1, NX):
-                x_copy(qbuf, q_send, q_recv, step, True).wait_recv()
-        else:
-            finish(chunk - 1)
-    finish(NCHUNK - 1)
+    for k in range(1, NEAR):
+        hear(k)
+    for chunk in chunks:
+        turn(chunk)
+        for step in Z_NEAR:
+            send_a(chunk, step).start()
+    for k in range(NEAR, 8):
+        hear(k)
+    for chunk in chunks:
+        for step in Z_FAR:
+            send_a(chunk, step).start()
+        first, end = CHUNKS[chunk]
+        x[my_z, first:end] = mid[my_z, first:end]
+
+    prepare(k1, b1, k2, b2, k3, b3, k4, sq, w1, w2, w3, b2c, k4c, p1f, p1b, p3h, p3l)
+
+    for step in range(1, NX):
+        x_copy(qbuf, q_send, q_recv, step, True).wait_recv()
+    for chunk in chunks:
+        for step in Z_NEAR + Z_FAR:
+            send_a(chunk, step, True).wait_recv()
+        gram_chunk(chunk, qbuf, x, best)
 
     qlen = qlen_ref[0]
     clen = clen_ref[cand_s[slab, pb]]
@@ -415,8 +422,8 @@
     )
     for step in range(1, NX):
         x_copy(scores, s_send, s_recv, step, False).start()
-    for chunk in range(NCHUNK):
-        for step in Z_ORDER:
+    for chunk in chunks:
+        for step in Z_NEAR + Z_FAR:
             send_a(chunk, step).wait_send()
         for step in range(1, NSLOT):
             send_b(chunk, step).wait_send()
@@ -467,25 +474,27 @@
         + [smem],
         out_specs=vmem,
         scratch_shapes=[
-            pltpu.VMEM((NCHUNK, SPER, 512, 256), BF),
-            pltpu.VMEM((NCHUNK, SPER, NZ, NSLOT, 256), BF),
-            pltpu.VMEM((NCHUNK, NZ, SPER, NSLOT, 256), BF),
-            pltpu.VMEM((NCHUNK, NSLOT, SPER, 2, 8, 256), BF),
-            pltpu.VMEM((NCHUNK, NSLOT, SPER, 2, 8, 256), BF),
+            pltpu.VMEM((9, 512, 256), BF),
+            pltpu.VMEM((NSLOT, 9, NZ, 256), BF),
+            pltpu.VMEM((NSLOT, 9, NZ, 256), BF),
+            pltpu.VMEM((NZ, 9, NSLOT, 256), BF),
+            pltpu.VMEM((NZ, 9, NSLOT, 256), BF),
             pltpu.VMEM((NX, 9, 4, 8, 256), BF),
         ]
         + compute_scratch()
         + [
             pltpu.VMEM((NX, 8, 128), F32),
-            dma((NCHUNK,)),
-            dma((NCHUNK, NZ)),
-            dma((NCHUNK, NZ)),
-            dma((NCHUNK, NSLOT)),
-            dma((NCHUNK, NSLOT)),
+            dma((len(CHUNKS),)),
+            dma((len(CHUNKS), NZ)),
+            dma((len(CHUNKS), NZ)),
+            dma((len(CHUNKS), NSLOT)),
+            dma((len(CHUNKS), NSLOT)),
             dma((NX,)),
             dma((NX,)),
             dma((NX,)),
             dma((NX,)),
+            pltpu.SemaphoreType.REGULAR((8,)),
+            pltpu.SemaphoreType.REGULAR((8,)),
         ],
         compiler_params=pltpu.CompilerParams(collective_id=0, has_side_effects=True),
         name="score_pairs",

time: 61.4 us -> 64.2 us (1.046)
  the two profiles are of different devices: /device:TPU:1 before, /device:TPU:24 now
where the time goes in v1:
time: 64.2 us; the launch traced here: 63.8 us
  Pallas kernels  61.3 us (95%)
  between operations  1.3 us (2%)
  local copies, waits for them, and re-layouts  1.19 us (2%)
    pallas_call x1, Pallas kernels, per_device(): pl.pallas_call(kernel, out_shape=jax.ShapeDtypeStruct((1, 4), F32), in_sp...  61.3 us

profile of v1, /device:TPU:24, one launch (start us, length us, event | category | flops | bytes accessed | tf_op | source)
XLA Modules:
  0.0 63.8 jit_solution(182458649310790557)
XLA Ops:
  1.3 61.3 %score_pairs.1 = f32[1,4]{1,0:T(1,128)} custom-call(bf16[9,32,256]{2,1,0:T(8,128)(2,1)} %bitcast.16, bf16[9,512,256]{2,1,0:T(8,128)(2,1)} %bitcast.14, s32[4,128]{1,0:T(4,128)} %bitcast.18, s32[4,128]{1,0:T(4,128)} %bitcast.19, s32[1]{0:T(128)S(6)} %copy.15.qlen_ref, s32[512]{0:T(512)} %clen_ref.1, f32[9,1,32]{2,1,0:T(1,128)} %bitcast.20, f32[1,32]{1,0:T(1,128)} %bitcast.21, ...), custom_call_target="tpu_custom_call" | custom-call | tf_op jit(solution)/shard_map/score_pairs/pallas_call | solution.py:469
  62.6 1.2 %copy.17 = f32[1,4]{1,0:T(1,128)} copy(f32[1,4]{1,0:T(1,128)} %score_pairs.1) | data formatting | bytes 32

commit v2 on v1

--- a/solution.py
+++ b/solution.py
@@ -9,13 +9,12 @@
 
 NY, NZ, NC, NX = 4, 16, 2, 4
 NSLOT = NY * NC
-CHUNKS = ((0, 2), (2, 5), (5, 9))
-NEAR = 3
+ALONG = ((0, 4),)
+ACROSS = ((4, 7), (7, 9))
 MESH = pl.DeviceIdType.MESH
 BF = jnp.bfloat16
 F32 = jnp.float32
-Z_NEAR = tuple(step for far in range(1, NEAR + 1) for step in (far, NZ - far))
-Z_FAR = (8,) + tuple(step for far in range(7, NEAR, -1) for step in (far, NZ - far))
+Z_ORDER = (8, 7, 9, 6, 10, 5, 11, 4, 12, 3, 13, 2, 14, 1, 15)
 
 
 def iota(shape, dim):
@@ -93,17 +92,13 @@
     p3l[576:640, :] = jnp.zeros((64, 1024), BF)
 
 
-def gram_chunk(chunk, qbuf, x, best):
-    first, end = CHUNKS[chunk]
-    p = iota((128, 128), 0)
-    source = (2 * (p & 7) + (p >> 6)) * NSLOT + ((p >> 5) & 1) * NY + ((p >> 3) & 3)
-    place = hot(iota((128, 128), 1) == source)
-    right = [dot(place, x[:, s].reshape(128, 256)).astype(BF) for s in range(first, end)]
+def gram_chunk(chunk, right, qbuf, best):
     right = jnp.concatenate(right, axis=0)
+    count = right.shape[0] // 128
     for r in range(9):
         g = dot_t(qbuf[:, r].reshape(128, 256), right)
         m = g[:, 0:128]
-        for s in range(1, end - first):
+        for s in range(1, count):
             m = jnp.maximum(m, g[:, s * 128 : s * 128 + 128])
         best[r] = m if chunk == 0 else jnp.maximum(best[r], m)
 
@@ -254,14 +249,16 @@
     return jnp.broadcast_to(score, (8, 128)) / number
 
 
-def kernel(
-    q_ref, f_ref, cand_v, cand_s, qlen_ref, clen_ref,
-    k1, b1, k2, b2, k3, b3, k4, b4,
-    out_ref,
-    frames, outgoing, landed, mid, x, qbuf, best, sq, w1, w2, w3, b2c, k4c,
-    p1f, p1b, p2h, p2l, p3h, p3l, scores,
-    f_sem, a_send, a_recv, b_send, b_recv, q_send, q_recv, s_send, s_recv, below, above,
-):
+def kernel(*refs):
+    operands, refs = refs[:14], refs[14:]
+    out_ref, refs = refs[0], refs[1:]
+    copies, refs = refs[:14], refs[14:]
+    (
+        zout, zin, smid, xs, sout, sin, zmid, xz, qbuf, best, sq, w1, w2, w3, b2c, k4c,
+        p1f, p1b, p2h, p2l, p3h, p3l, scores,
+        in_sem, f_sem, a_send, a_recv, b_send, b_recv, q_send, q_recv, s_send, s_recv,
+    ) = refs
+    q_ref, frames, cand_v, cand_s, qlen_ref, clen_ref, k1, b1, k2, b2, k3, b3, k4, b4 = copies
     pb = lax.axis_index("pb")
     slab = lax.axis_index("slab")
     my_y = lax.div(pb, NZ * NC)
@@ -283,56 +280,63 @@
         return other, (pb, other)
 
     barrier = pltpu.get_barrier_semaphore()
-    near = [z_peer(1), z_peer(NZ - 1)]
-    near += [slot_peer(step) for step in range(1, NSLOT)]
-    near += [x_peer(step) for step in range(1, NX)]
-    for _, device in near:
+    peers = [z_peer(step) for step in Z_ORDER]
+    peers += [slot_peer(step) for step in range(1, NSLOT)]
+    peers += [x_peer(step) for step in range(1, NX)]
+    for _, device in peers:
         pl.semaphore_signal(barrier, inc=1, device_id=device, device_id_type=MESH)
 
+    chunks = ALONG + ACROSS
+
     def fetch(chunk):
-        first, end = CHUNKS[chunk]
+        first, end = chunks[chunk]
         regions = pl.ds(first, end - first)
-        return pltpu.make_async_copy(f_ref.at[regions], frames.at[regions], f_sem.at[chunk])
-
-    chunks = range(len(CHUNKS))
-    for chunk in chunks:
+        return pltpu.make_async_copy(
+            operands[1].at[regions], frames.at[regions], f_sem.at[chunk]
+        )
+
+    def bring(i):
+        return pltpu.make_async_copy(operands[i], copies[i], in_sem.at[i])
+
+    bring(2).start()
+    for chunk in range(len(chunks)):
         fetch(chunk).start()
+    others = (0, 3, 4, 5, 6, 7, 8, 9, 10, 11, 12, 13)
+    for i in others:
+        bring(i).start()
 
     n = iota((128, 128), 0)
-    asks = (((n >> 4) & 3) * NZ + (n & 15)) * NC + (n >> 6)
-    order = hot(iota((128, 128), 1) == asks)
+    lane = iota((128, 128), 1)
+    zs = hot(lane == ((n & 3) * NZ + (n >> 3)) * NC + ((n >> 2) & 1))
+    sz = hot(lane == (((n >> 4) & 3) * NZ + (n & 15)) * NC + (n >> 6))
+    bring(2).wait()
     wanted = jnp.broadcast_to(cand_v[pl.ds(slab, 1), :], (512, 128))
-    select = dot_t(order, hot(iota((512, 128), 0) == wanted)).astype(BF)
-
-    def gather(chunk):
-        fetch(chunk).wait()
-        for s in range(*CHUNKS[chunk]):
-            outgoing[:, s] = dot(select, frames[s]).reshape(NSLOT, NZ, 256).astype(BF)
-
-    def send_b(chunk, step, arriving=False):
-        first, end = CHUNKS[chunk]
+    wanted = hot(iota((512, 128), 0) == wanted)
+
+    def z_copy(chunk, step, src, dst, arriving=False):
+        first, end = chunks[chunk]
+        regions = pl.ds(first, end - first)
+        z, device = z_peer(step)
+        place = z if arriving else my_z
+        return pltpu.make_async_remote_copy(
+            src_ref=src.at[z, regions],
+            dst_ref=dst.at[place, regions],
+            send_sem=a_send.at[chunk, step],
+            recv_sem=a_recv.at[chunk, place],
+            device_id=device,
+            device_id_type=MESH,
+        )
+
+    def s_copy(chunk, step, src, dst, arriving=False):
+        first, end = chunks[chunk]
         regions = pl.ds(first, end - first)
         slot, device = slot_peer(step)
         place = slot if arriving else my_slot
         return pltpu.make_async_remote_copy(
-            src_ref=outgoing.at[slot, regions],
-            dst_ref=landed.at[place, regions],
+            src_ref=src.at[slot, regions],
+            dst_ref=dst.at[place, regions],
             send_sem=b_send.at[chunk, step],
             recv_sem=b_recv.at[chunk, place],
-            device_id=device,
-            device_id_type=MESH,
-        )
-
-    def send_a(chunk, step, arriving=False):
-        first, end = CHUNKS[chunk]
-        regions = pl.ds(first, end - first)
-        z, device = z_peer(step)
-        place = z if arriving else my_z
-        return pltpu.make_async_remote_copy(
-            src_ref=mid.at[z, regions],
-            dst_ref=x.at[place, regions],
-            send_sem=a_send.at[chunk, step],
-            recv_sem=a_recv.at[chunk, place],
             device_id=device,
             device_id_type=MESH,
         )
@@ -349,71 +353,95 @@
             device_id_type=MESH,
         )
 
-    def tell(k):
-        if k <= 7:
-            pl.semaphore_signal(
-                below.at[k], inc=1, device_id=z_peer(1)[1], device_id_type=MESH
-            )
-        if k <= 6:
-            pl.semaphore_signal(
-                above.at[k], inc=1, device_id=z_peer(NZ - 1)[1], device_id_type=MESH
-            )
-
-    def hear(k):
-        pl.semaphore_wait(below.at[k], 1)
-        if k <= 6:
-            pl.semaphore_wait(above.at[k], 1)
-        tell(k + 1)
-
-    m = iota((128, 128), 0)
-    shuffle = hot(iota((128, 128), 1) == (m & 7) * NZ + (m >> 3))
-
-    def turn(chunk):
-        first, end = CHUNKS[chunk]
-        landed[my_slot, first:end] = outgoing[my_slot, first:end]
+    def z_start(chunk, src, dst):
+        for step in Z_ORDER:
+            z_copy(chunk, step, src, dst).start()
+        first, end = chunks[chunk]
+        dst[my_z, first:end] = src[my_z, first:end]
+
+    def s_start(chunk, src, dst):
         for step in range(1, NSLOT):
-            send_b(chunk, step, True).wait_recv()
-        for s in range(first, end):
-            rows = dot(shuffle, landed[:, s].reshape(128, 256))
-            mid[:, s] = rows.reshape(NZ, NSLOT, 256).astype(BF)
-
-    gather(0)
-    pl.semaphore_wait(barrier, len(near))
-    tell(1)
-    for step in range(1, NSLOT):
-        send_b(0, step).start()
+            s_copy(chunk, step, src, dst).start()
+        first, end = chunks[chunk]
+        dst[my_slot, first:end] = src[my_slot, first:end]
+
+    def z_wait(chunk, src, dst):
+        for step in Z_ORDER:
+            z_copy(chunk, step, src, dst, True).wait_recv()
+
+    def s_wait(chunk, src, dst):
+        for step in range(1, NSLOT):
+            s_copy(chunk, step, src, dst, True).wait_recv()
+
+    along = range(len(ALONG))
+    across = range(len(ALONG), len(chunks))
+
+    def gather_along(chunk):
+        fetch(chunk).wait()
+        for s in range(*chunks[chunk]):
+            zout[:, s] = dot(by_z, frames[s]).reshape(NZ, NSLOT, 256).astype(BF)
+
+    def gather_across(chunk):
+        fetch(chunk).wait()
+        for s in range(*chunks[chunk]):
+            sout[:, s] = dot(by_slot, frames[s]).reshape(NSLOT, NZ, 256).astype(BF)
+
+    by_z = dot_t(zs, wanted).astype(BF)
+    for chunk in along:
+        gather_along(chunk)
+    by_slot = dot_t(sz, wanted).astype(BF)
+    bring(0).wait()
     qi = iota((32, 32), 0)
     pick = hot(iota((32, 32), 1) == 4 * (qi & 7) + (qi >> 3))
     for r in range(9):
         qbuf[slab, r] = dot(pick, q_ref[r]).reshape(4, 8, 256).astype(BF)
+    for chunk in across:
+        gather_across(chunk)
+
+    pl.semaphore_wait(barrier, len(peers))
+    for chunk in along:
+        z_start(chunk, zout, zin)
+    for chunk in across:
+        s_start(chunk, sout, sin)
     for step in range(1, NX):
         x_copy(qbuf, q_send, q_recv, step, False).start()
-    for chunk in chunks[1:]:
-        gather(chunk)
-        for step in range(1, NSLOT):
-            send_b(chunk, step).start()
-    for k in range(1, NEAR):
-        hear(k)
-    for chunk in chunks:
-        turn(chunk)
-        for step in Z_NEAR:
-            send_a(chunk, step).start()
-    for k in range(NEAR, 8):
-        hear(k)
-    for chunk in chunks:
-        for step in Z_FAR:
-            send_a(chunk, step).start()
-        first, end = CHUNKS[chunk]
-        x[my_z, first:end] = mid[my_z, first:end]
+    for i in others[1:]:
+        bring(i).wait()
+
+    to_z = hot(lane == (n & 7) * NZ + (n >> 3))
+    to_slot = hot(lane == (2 * (n & 7) + ((n >> 3) & 1)) * NSLOT + (n >> 4))
+    place = hot(
+        lane == (2 * (n & 7) + (n >> 6)) * NSLOT + ((n >> 5) & 1) * NY + ((n >> 3) & 3)
+    )
+    for chunk in across:
+        s_wait(chunk, sout, sin)
+        for s in range(*chunks[chunk]):
+            rows = dot(to_z, sin[:, s].reshape(128, 256))
+            zmid[:, s] = rows.reshape(NZ, NSLOT, 256).astype(BF)
+        z_start(chunk, zmid, xz)
 
     prepare(k1, b1, k2, b2, k3, b3, k4, sq, w1, w2, w3, b2c, k4c, p1f, p1b, p3h, p3l)
 
+    for chunk in along:
+        z_wait(chunk, zout, zin)
+        for s in range(*chunks[chunk]):
+            rows = dot(to_slot, zin[:, s].reshape(128, 256))
+            smid[:, s] = rows.reshape(NSLOT, 2, 8, 256).astype(BF)
+        s_start(chunk, smid, xs)
     for step in range(1, NX):
         x_copy(qbuf, q_send, q_recv, step, True).wait_recv()
-    for chunk in chunks:
-        for step in Z_NEAR + Z_FAR:
-            send_a(chunk, step, True).wait_recv()
-        gram_chunk(chunk, qbuf, x, best)
+    for chunk in along:
+        s_wait(chunk, smid, xs)
+        right = [
+            xs[:, s, e].reshape(64, 256) for s in range(*chunks[chunk]) for e in range(2)
+        ]
+        gram_chunk(chunk, right, qbuf, best)
+    for chunk in across:
+        z_wait(chunk, zmid, xz)
+        right = [
+            dot(place, xz[:, s].reshape(128, 256)).astype(BF) for s in range(*chunks[chunk])
+        ]
+        gram_chunk(chunk, right, qbuf, best)
 
     qlen = qlen_ref[0]
     clen = clen_ref[cand_s[slab, pb]]
@@ -422,11 +450,12 @@
     )
     for step in range(1, NX):
         x_copy(scores, s_send, s_recv, step, False).start()
-    for chunk in chunks:
-        for step in Z_NEAR + Z_FAR:
-            send_a(chunk, step).wait_send()
+    for chunk in range(len(chunks)):
+        line, pair = ((zout, zin), (smid, xs)) if chunk in along else ((zmid, xz), (sout, sin))
+        for step in Z_ORDER:
+            z_copy(chunk, step, *line).wait_send()
         for step in range(1, NSLOT):
-            send_b(chunk, step).wait_send()
+            s_copy(chunk, step, *pair).wait_send()
     for step in range(1, NX):
         x_copy(qbuf, q_send, q_recv, step, False).wait_send()
     for step in range(1, NX):
@@ -463,38 +492,48 @@
     kernel_one, bias_one, kernel_two, bias_two, kernel_three, bias_three, kernel_four, bias_four,
 ):
     vmem = pl.BlockSpec(memory_space=pltpu.VMEM)
-    smem = pl.BlockSpec(memory_space=pltpu.SMEM)
     dma = pltpu.SemaphoreType.DMA
+    count = len(ALONG + ACROSS)
     pairs = candidates.T
+    by_z = pltpu.VMEM((NZ, 9, NSLOT, 256), BF)
+    by_slot = pltpu.VMEM((NSLOT, 9, NZ, 256), BF)
+    to_gram = pltpu.VMEM((NSLOT, 9, 2, 8, 256), BF)
     return pl.pallas_call(
         kernel,
         out_shape=jax.ShapeDtypeStruct((1, 4), F32),
-        in_specs=[vmem, pl.BlockSpec(memory_space=pl.ANY), vmem, smem, smem, smem]
-        + [vmem] * 7
-        + [smem],
+        in_specs=[pl.BlockSpec(memory_space=pl.ANY)] * 14,
         out_specs=vmem,
         scratch_shapes=[
+            pltpu.VMEM((9, 32, 256), BF),
             pltpu.VMEM((9, 512, 256), BF),
-            pltpu.VMEM((NSLOT, 9, NZ, 256), BF),
-            pltpu.VMEM((NSLOT, 9, NZ, 256), BF),
-            pltpu.VMEM((NZ, 9, NSLOT, 256), BF),
-            pltpu.VMEM((NZ, 9, NSLOT, 256), BF),
+            pltpu.VMEM((4, 128), jnp.int32),
+            pltpu.SMEM((4, 128), jnp.int32),
+            pltpu.SMEM((1,), jnp.int32),
+            pltpu.SMEM((512,), jnp.int32),
+            pltpu.VMEM((9, 1, 32), F32),
+            pltpu.VMEM((1, 32), F32),
+            pltpu.VMEM((288, 64), F32),
+            pltpu.VMEM((1, 64), F32),
+            pltpu.VMEM((576, 128), F32),
+            pltpu.VMEM((1, 128), F32),
+            pltpu.VMEM((1, 128), F32),
+            pltpu.SMEM((1,), F32),
+            by_z, by_z, to_gram, to_gram, by_slot, by_slot, by_z, by_z,
             pltpu.VMEM((NX, 9, 4, 8, 256), BF),
         ]
         + compute_scratch()
         + [
             pltpu.VMEM((NX, 8, 128), F32),
-            dma((len(CHUNKS),)),
-            dma((len(CHUNKS), NZ)),
-            dma((len(CHUNKS), NZ)),
-            dma((len(CHUNKS), NSLOT)),
-            dma((len(CHUNKS), NSLOT)),
+            dma((14,)),
+            dma((count,)),
+            dma((count, NZ)),
+            dma((count, NZ)),
+            dma((count, NSLOT)),
+            dma((count, NSLOT)),
             dma((NX,)),
             dma((NX,)),
             dma((NX,)),
             dma((NX,)),
-            pltpu.SemaphoreType.REGULAR((8,)),
-            pltpu.SemaphoreType.REGULAR((8,)),
         ],
         compiler_params=pltpu.CompilerParams(collective_id=0, has_side_effects=True),
         name="score_pairs",

time: 64.2 us -> 55.6 us (0.87)
  Pallas kernels: 61.3 us -> 52.9 us
    pallas_call x1, Pallas kernels: 61.3 us -> 52.9 us  [per_device(): pl.pallas_call(kernel, out_shape=jax.ShapeDtypeStruct((1, 4), F32), in_sp...]
where the time goes in v2:
time: 55.6 us; the launch traced here: 55.4 us
  Pallas kernels  52.9 us (95%)
  between operations  1.3 us (2%)
  local copies, waits for them, and re-layouts  1.19 us (2%)
    pallas_call x1, Pallas kernels, per_device(): pl.pallas_call(kernel, out_shape=jax.ShapeDtypeStruct((1, 4), F32), in_sp...  52.9 us
    unnamed x1, local copies, waits for them, and re-layouts  1.19 us

profile of v2, /device:TPU:24, one launch (start us, length us, event | category | flops | bytes accessed | tf_op | source)
XLA Modules:
  0.0 55.4 jit_solution(9279115465184428699)
XLA Ops:
  1.3 52.9 %score_pairs.1 = f32[1,4]{1,0:T(1,128)} custom-call(bf16[9,32,256]{2,1,0:T(8,128)(2,1)} %bitcast.16, bf16[9,512,256]{2,1,0:T(8,128)(2,1)} %bitcast.14, s32[4,128]{1,0:T(4,128)} %bitcast.18, s32[4,128]{1,0:T(4,128)} %bitcast.19, s32[1]{0:T(128)S(6)} %copy.15.refs_4_, s32[512]{0:T(512)} %refs_5_.1, f32[9,1,32]{2,1,0:T(1,128)} %bitcast.20, f32[1,32]{1,0:T(1,128)} %bitcast.21, ...), custom_call_target="tpu_custom_call" | custom-call | tf_op jit(solution)/shard_map/score_pairs/pallas_call | solution.py:501
  54.2 1.2 %copy.17 = f32[1,4]{1,0:T(1,128)} copy(f32[1,4]{1,0:T(1,128)} %score_pairs.1) | data formatting | bytes 32

commit v3 on v2

--- a/solution.py
+++ b/solution.py
@@ -9,8 +9,8 @@
 
 NY, NZ, NC, NX = 4, 16, 2, 4
 NSLOT = NY * NC
-ALONG = ((0, 4),)
-ACROSS = ((4, 7), (7, 9))
+ALONG = ((0, 5),)
+ACROSS = ((5, 9),)
 MESH = pl.DeviceIdType.MESH
 BF = jnp.bfloat16
 F32 = jnp.float32

time: 55.6 us -> 54.7 us (0.984)
  Pallas kernels: 52.9 us -> 52 us
    pallas_call x1, Pallas kernels: 52.9 us -> 52 us  [per_device(): pl.pallas_call(kernel, out_shape=jax.ShapeDtypeStruct((1, 4), F32), in_sp...]
where the time goes in v3:
time: 54.7 us; the launch traced here: 54.5 us
  Pallas kernels  52 us (95%)
  between operations  1.3 us (2%)
  local copies, waits for them, and re-layouts  1.19 us (2%)
    pallas_call x1, Pallas kernels, per_device(): pl.pallas_call(kernel, out_shape=jax.ShapeDtypeStruct((1, 4), F32), in_sp...  52 us
    unnamed x1, local copies, waits for them, and re-layouts  1.19 us

profile of v3, /device:TPU:24, one launch (start us, length us, event | category | flops | bytes accessed | tf_op | source)
XLA Modules:
  0.0 54.5 jit_solution(921027414386414661)
XLA Ops:
  1.3 52.0 %score_pairs.1 = f32[1,4]{1,0:T(1,128)} custom-call(bf16[9,32,256]{2,1,0:T(8,128)(2,1)} %bitcast.16, bf16[9,512,256]{2,1,0:T(8,128)(2,1)} %bitcast.14, s32[4,128]{1,0:T(4,128)} %bitcast.18, s32[4,128]{1,0:T(4,128)} %bitcast.19, s32[1]{0:T(128)S(6)} %copy.15.refs_4_, s32[512]{0:T(512)} %refs_5_.1, f32[9,1,32]{2,1,0:T(1,128)} %bitcast.20, f32[1,32]{1,0:T(1,128)} %bitcast.21, ...), custom_call_target="tpu_custom_call" | custom-call | tf_op jit(solution)/shard_map/score_pairs/pallas_call | solution.py:501
  53.3 1.2 %copy.17 = f32[1,4]{1,0:T(1,128)} copy(f32[1,4]{1,0:T(1,128)} %score_pairs.1) | data formatting | bytes 32

commit v4 on v3

--- a/solution.py
+++ b/solution.py
@@ -39,7 +39,7 @@
     return hi, lo
 
 
-def prepare(k1, b1, k2, b2, k3, b3, k4, sq, w1, w2, w3, b2c, k4c, p1f, p1b, p3h, p3l):
+def prepare(k1, b1, k2, b2, k3, b3, k4, sq, w1, w2, w3, b2c, k4c, p1f, p1b):
     sq[...] = jnp.zeros_like(sq)
     for tap in range(9):
         sq[tap : tap + 1, 0:32] = k1[tap]
@@ -88,8 +88,6 @@
     ones = jnp.where(iota((16, 128), 0) == 4, 1.0, 0.0)
     for u in range(8):
         p1f[u * 48 + 32 : u * 48 + 48, :] = ones
-    p3h[576:640, :] = hot(iota((64, 1024), 0) == 0)
-    p3l[576:640, :] = jnp.zeros((64, 1024), BF)
 
 
 def gram_chunk(chunk, right, qbuf, best):
@@ -169,25 +167,20 @@
     grp32, col32 = tall(grp, 32), tall(col, 32)
     grp64, col64 = tall(grp, 64), tall(col, 64)
 
-    def put(high, low, at, n, u, value):
+    def put(high, low, at, n, tile, value):
         hi, lo = halves(value)
-        high[at : at + n, u * 128 : u * 128 + 128] = hi
-        low[at : at + n, u * 128 : u * 128 + 128] = lo
-        return hi, lo
-
-    def put_above(high, low, at, n, u, value, pair, groups):
-        if u < 7:
-            high[at : at + n, u * 128 + 128 : u * 128 + 256] = pair[0]
-            low[at : at + n, u * 128 + 128 : u * 128 + 256] = pair[1]
-        else:
-            put(high, low, at, n, 0, jnp.where(groups == 0, 0.0, pltpu.roll(value, 32, 1)))
-
-    def put_below(high, low, at, n, u, value, pair, groups):
-        if u > 0:
-            high[at : at + n, u * 128 - 128 : u * 128] = pair[0]
-            low[at : at + n, u * 128 - 128 : u * 128] = pair[1]
-        else:
-            put(high, low, at, n, 7, jnp.where(groups == 3, 0.0, pltpu.roll(value, 96, 1)))
+        high[at : at + n, tile * 128 : tile * 128 + 128] = hi
+        low[at : at + n, tile * 128 : tile * 128 + 128] = lo
+
+    def put_before(high, low, at, n, value, groups):
+        put(high, low, at, n, 0, jnp.where(groups == 0, 0.0, pltpu.roll(value, 32, 1)))
+
+    def put_after(high, low, at, n, value, groups):
+        put(high, low, at, n, 9, jnp.where(groups == 3, 0.0, pltpu.roll(value, 96, 1)))
+
+    def window(ref, first, end, tile, move):
+        at = (tile * 2 + 1 + move) * 128
+        return ref[first:end, at : at + 256]
 
     for tile in range(4):
         o1 = dot(w1[...], p1b[:, tile * 256 : tile * 256 + 256])
@@ -208,16 +201,26 @@
                     moved = jnp.where(col32 == 31, 0.0, pltpu.roll(v, 127, 1))
                     variants = ((1, v), (3, moved))
                 for e, w in variants:
-                    if a == 0:
-                        pair = put(p2h, p2l, (4 + e) * 32, 32, u, w)
-                        put_below(p2h, p2l, (12 + e) * 32, 32, u, w, pair, grp32)
-                    else:
-                        pair = put(p2h, p2l, (8 + e) * 32, 32, u, w)
-                        put_above(p2h, p2l, e * 32, 32, u, w, pair, grp32)
+                    at = (a * 4 + e) * 32
+                    put(p2h, p2l, at, 32, u + 1, w)
+                    if a == 0 and u == 0:
+                        put_after(p2h, p2l, at, 32, w, grp32)
+                    if a == 1 and u == 7:
+                        put_before(p2h, p2l, at, 32, w, grp32)
     for tile in range(4):
-        lanes = slice(tile * 256, tile * 256 + 256)
-        first = dot(w2[...], p2h[:, lanes])
-        o2 = first[0:256] + (first[256:512] + dot(w2[0:256, :], p2l[:, lanes]))
+        high, low = (
+            jnp.concatenate(
+                [
+                    window(ref, 128, 256, tile, -1),
+                    window(ref, 0, 256, tile, 0),
+                    window(ref, 0, 128, tile, 1),
+                ],
+                axis=0,
+            )
+            for ref in (p2h, p2l)
+        )
+        first = dot(w2[...], high)
+        o2 = first[0:256] + (first[256:512] + dot(w2[0:256, :], low))
         m = jnp.maximum(
             jnp.maximum(o2[0:64], o2[64:128]), jnp.maximum(o2[128:192], o2[192:256])
         )
@@ -227,14 +230,22 @@
             left = jnp.where(col64 == 0, 0.0, pltpu.roll(v, 1, 1))
             right = jnp.where(col64 == 31, 0.0, pltpu.roll(v, 127, 1))
             for dj, w in ((0, left), (1, v), (2, right)):
-                pair = put(p3h, p3l, (3 + dj) * 64, 64, u, w)
-                put_above(p3h, p3l, dj * 64, 64, u, w, pair, grp64)
-                put_below(p3h, p3l, (6 + dj) * 64, 64, u, w, pair, grp64)
+                put(p3h, p3l, dj * 64, 64, u + 1, w)
+                if u == 0:
+                    put_after(p3h, p3l, dj * 64, 64, w, grp64)
+                if u == 7:
+                    put_before(p3h, p3l, dj * 64, 64, w, grp64)
     final = []
+    one = hot(iota((64, 256), 0) == 0)
     for tile in range(4):
-        lanes = slice(tile * 256, tile * 256 + 256)
-        first = dot(w3[...], p3h[:, lanes])
-        o3 = first[0:128] + (first[128:256] + dot(w3[0:128, :], p3l[:, lanes]))
+        high, low = (
+            jnp.concatenate(
+                [window(ref, 0, 192, tile, move) for move in (-1, 0, 1)] + last, axis=0
+            )
+            for ref, last in ((p3h, [one]), (p3l, [jnp.zeros_like(one)]))
+        )
+        first = dot(w3[...], high)
+        o3 = first[0:128] + (first[128:256] + dot(w3[0:128, :], low))
         o3 = jnp.maximum(o3, 0.0)
         for half in range(2):
             v = o3[:, half * 128 : half * 128 + 128] * k4c[...]
@@ -313,42 +324,39 @@
     wanted = jnp.broadcast_to(cand_v[pl.ds(slab, 1), :], (512, 128))
     wanted = hot(iota((512, 128), 0) == wanted)
 
-    def z_copy(chunk, step, src, dst, arriving=False):
+    def z_copy(chunk, step, src, dst):
         first, end = chunks[chunk]
         regions = pl.ds(first, end - first)
         z, device = z_peer(step)
-        place = z if arriving else my_z
         return pltpu.make_async_remote_copy(
             src_ref=src.at[z, regions],
-            dst_ref=dst.at[place, regions],
-            send_sem=a_send.at[chunk, step],
-            recv_sem=a_recv.at[chunk, place],
+            dst_ref=dst.at[my_z, regions],
+            send_sem=a_send.at[chunk],
+            recv_sem=a_recv.at[chunk],
             device_id=device,
             device_id_type=MESH,
         )
 
-    def s_copy(chunk, step, src, dst, arriving=False):
+    def s_copy(chunk, step, src, dst):
         first, end = chunks[chunk]
         regions = pl.ds(first, end - first)
         slot, device = slot_peer(step)
-        place = slot if arriving else my_slot
         return pltpu.make_async_remote_copy(
             src_ref=src.at[slot, regions],
-            dst_ref=dst.at[place, regions],
-            send_sem=b_send.at[chunk, step],
-            recv_sem=b_recv.at[chunk, place],
+            dst_ref=dst.at[my_slot, regions],
+            send_sem=b_send.at[chunk],
+            recv_sem=b_recv.at[chunk],
             device_id=device,
             device_id_type=MESH,
         )
 
-    def x_copy(buffer, send, recv, step, arriving):
+    def x_copy(buffer, send, recv, step):
         other, device = x_peer(step)
-        place = other if arriving else slab
         return pltpu.make_async_remote_copy(
             src_ref=buffer.at[slab],
-            dst_ref=buffer.at[place],
-            send_sem=send.at[step],
-            recv_sem=recv.at[place],
+            dst_ref=buffer.at[slab],
+            send_sem=send.at[0],
+            recv_sem=recv.at[0],
             device_id=device,
             device_id_type=MESH,
         )
@@ -365,13 +373,37 @@
         first, end = chunks[chunk]
         dst[my_slot, first:end] = src[my_slot, first:end]
 
-    def z_wait(chunk, src, dst):
-        for step in Z_ORDER:
-            z_copy(chunk, step, src, dst, True).wait_recv()
-
-    def s_wait(chunk, src, dst):
-        for step in range(1, NSLOT):
-            s_copy(chunk, step, src, dst, True).wait_recv()
+    def z_group(chunk, src, dst):
+        first, end = chunks[chunk]
+        return pltpu.make_async_remote_copy(
+            src_ref=src.at[pl.ds(0, NZ - 1), pl.ds(first, end - first)],
+            dst_ref=dst.at[pl.ds(0, NZ - 1), pl.ds(first, end - first)],
+            send_sem=a_send.at[chunk],
+            recv_sem=a_recv.at[chunk],
+            device_id=z_peer(1)[1],
+            device_id_type=MESH,
+        )
+
+    def s_group(chunk, src, dst):
+        first, end = chunks[chunk]
+        return pltpu.make_async_remote_copy(
+            src_ref=src.at[pl.ds(0, NSLOT - 1), pl.ds(first, end - first)],
+            dst_ref=dst.at[pl.ds(0, NSLOT - 1), pl.ds(first, end - first)],
+            send_sem=b_send.at[chunk],
+            recv_sem=b_recv.at[chunk],
+            device_id=slot_peer(1)[1],
+            device_id_type=MESH,
+        )
+
+    def x_group(buffer, send, recv):
+        return pltpu.make_async_remote_copy(
+            src_ref=buffer.at[pl.ds(0, NX - 1)],
+            dst_ref=buffer.at[pl.ds(0, NX - 1)],
+            send_sem=send.at[0],
+            recv_sem=recv.at[0],
+            device_id=x_peer(1)[1],
+            device_id_type=MESH,
+        )
 
     along = range(len(ALONG))
     across = range(len(ALONG), len(chunks))
@@ -404,7 +436,7 @@
     for chunk in across:
         s_start(chunk, sout, sin)
     for step in range(1, NX):
-        x_copy(qbuf, q_send, q_recv, step, False).start()
+        x_copy(qbuf, q_send, q_recv, step).start()
     for i in others[1:]:
         bring(i).wait()
 
@@ -414,30 +446,29 @@
         lane == (2 * (n & 7) + (n >> 6)) * NSLOT + ((n >> 5) & 1) * NY + ((n >> 3) & 3)
     )
     for chunk in across:
-        s_wait(chunk, sout, sin)
+        s_group(chunk, sout, sin).wait_recv()
         for s in range(*chunks[chunk]):
             rows = dot(to_z, sin[:, s].reshape(128, 256))
             zmid[:, s] = rows.reshape(NZ, NSLOT, 256).astype(BF)
         z_start(chunk, zmid, xz)
 
-    prepare(k1, b1, k2, b2, k3, b3, k4, sq, w1, w2, w3, b2c, k4c, p1f, p1b, p3h, p3l)
+    prepare(k1, b1, k2, b2, k3, b3, k4, sq, w1, w2, w3, b2c, k4c, p1f, p1b)
 
     for chunk in along:
-        z_wait(chunk, zout, zin)
+        z_group(chunk, zout, zin).wait_recv()
         for s in range(*chunks[chunk]):
             rows = dot(to_slot, zin[:, s].reshape(128, 256))
             smid[:, s] = rows.reshape(NSLOT, 2, 8, 256).astype(BF)
         s_start(chunk, smid, xs)
-    for step in range(1, NX):
-        x_copy(qbuf, q_send, q_recv, step, True).wait_recv()
+    x_group(qbuf, q_send, q_recv).wait_recv()
     for chunk in along:
-        s_wait(chunk, smid, xs)
+        s_group(chunk, smid, xs).wait_recv()
         right = [
             xs[:, s, e].reshape(64, 256) for s in range(*chunks[chunk]) for e in range(2)
         ]
         gram_chunk(chunk, right, qbuf, best)
     for chunk in across:
-        z_wait(chunk, zmid, xz)
+        z_group(chunk, zmid, xz).wait_recv()
         right = [
             dot(place, xz[:, s].reshape(128, 256)).astype(BF) for s in range(*chunks[chunk])
         ]
@@ -449,19 +480,14 @@
         best, qlen, clen, b4[0], w1, w2, w3, b2c, k4c, p1f, p1b, p2h, p2l, p3h, p3l
     )
     for step in range(1, NX):
-        x_copy(scores, s_send, s_recv, step, False).start()
+        x_copy(scores, s_send, s_recv, step).start()
     for chunk in range(len(chunks)):
         line, pair = ((zout, zin), (smid, xs)) if chunk in along else ((zmid, xz), (sout, sin))
-        for step in Z_ORDER:
-            z_copy(chunk, step, *line).wait_send()
-        for step in range(1, NSLOT):
-            s_copy(chunk, step, *pair).wait_send()
-    for step in range(1, NX):
-        x_copy(qbuf, q_send, q_recv, step, False).wait_send()
-    for step in range(1, NX):
-        x_copy(scores, s_send, s_recv, step, True).wait_recv()
-    for step in range(1, NX):
-        x_copy(scores, s_send, s_recv, step, False).wait_send()
+        z_group(chunk, *line).wait_send()
+        s_group(chunk, *pair).wait_send()
+    x_group(qbuf, q_send, q_recv).wait_send()
+    x_group(scores, s_send, s_recv).wait_send()
+    x_group(scores, s_send, s_recv).wait_recv()
     where = iota((1, 128), 1)
     line = scores[0, 0:1]
     for other in range(1, NX):
@@ -480,10 +506,10 @@
         pltpu.VMEM((128, 128), F32),
         pltpu.VMEM((384, 128), F32),
         pltpu.VMEM((256, 1024), BF),
-        pltpu.VMEM((512, 1024), BF),
-        pltpu.VMEM((512, 1024), BF),
-        pltpu.VMEM((640, 1024), BF),
-        pltpu.VMEM((640, 1024), BF),
+        pltpu.VMEM((256, 1280), BF),
+        pltpu.VMEM((256, 1280), BF),
+        pltpu.VMEM((192, 1280), BF),
+        pltpu.VMEM((192, 1280), BF),
     ]
 
 
@@ -526,14 +552,14 @@
             pltpu.VMEM((NX, 8, 128), F32),
             dma((14,)),
             dma((count,)),
-            dma((count, NZ)),
-            dma((count, NZ)),
-            dma((count, NSLOT)),
-            dma((count, NSLOT)),
-            dma((NX,)),
-            dma((NX,)),
-            dma((NX,)),
-            dma((NX,)),
+            dma((count,)),
+            dma((count,)),
+            dma((count,)),
+            dma((count,)),
+            dma((1,)),
+            dma((1,)),
+            dma((1,)),
+            dma((1,)),
         ],
         compiler_params=pltpu.CompilerParams(collective_id=0, has_side_effects=True),
         name="score_pairs",

time: 54.7 us -> 53.7 us (0.982)
  Pallas kernels: 52 us -> 51.1 us
    pallas_call x1, Pallas kernels: 52 us -> 51.1 us  [per_device(): pl.pallas_call(kernel, out_shape=jax.ShapeDtypeStruct((1, 4), F32), in_sp...]
where the time goes in v4:
time: 53.7 us; the launch traced here: 53.6 us
  Pallas kernels  51.1 us (95%)
  between operations  1.3 us (2%)
  local copies, waits for them, and re-layouts  1.19 us (2%)
    pallas_call x1, Pallas kernels, per_device(): pl.pallas_call(kernel, out_shape=jax.ShapeDtypeStruct((1, 4), F32), in_sp...  51.1 us
    unnamed x1, local copies, waits for them, and re-layouts  1.19 us

profile of v4, /device:TPU:24, one launch (start us, length us, event | category | flops | bytes accessed | tf_op | source)
XLA Modules:
  0.0 53.6 jit_solution(12302763618789487036)
XLA Ops:
  1.3 51.1 %score_pairs.1 = f32[1,4]{1,0:T(1,128)} custom-call(bf16[9,32,256]{2,1,0:T(8,128)(2,1)} %bitcast.16, bf16[9,512,256]{2,1,0:T(8,128)(2,1)} %bitcast.14, s32[4,128]{1,0:T(4,128)} %bitcast.18, s32[4,128]{1,0:T(4,128)} %bitcast.19, s32[1]{0:T(128)S(6)} %copy.15.refs_4_, s32[512]{0:T(512)} %refs_5_.1, f32[9,1,32]{2,1,0:T(1,128)} %bitcast.20, f32[1,32]{1,0:T(1,128)} %bitcast.21, ...), custom_call_target="tpu_custom_call" | custom-call | tf_op jit(solution)/shard_map/score_pairs/pallas_call | solution.py:527
  52.4 1.2 %copy.17 = f32[1,4]{1,0:T(1,128)} copy(f32[1,4]{1,0:T(1,128)} %score_pairs.1) | data formatting | bytes 32

commit v5 on v4

--- a/solution.py
+++ b/solution.py
@@ -431,10 +431,10 @@
         gather_across(chunk)
 
     pl.semaphore_wait(barrier, len(peers))
+    for chunk in across:
+        s_start(chunk, sout, sin)
     for chunk in along:
         z_start(chunk, zout, zin)
-    for chunk in across:
-        s_start(chunk, sout, sin)
     for step in range(1, NX):
         x_copy(qbuf, q_send, q_recv, step).start()
     for i in others[1:]:

time: 53.7 us -> 53.8 us (level)
  no operation moved by 1% of the time
where the time goes in v5:
time: 53.8 us; the launch traced here: 53.6 us
  Pallas kernels  51.1 us (95%)
  between operations  1.3 us (2%)
  local copies, waits for them, and re-layouts  1.19 us (2%)
    pallas_call x1, Pallas kernels, per_device(): pl.pallas_call(kernel, out_shape=jax.ShapeDtypeStruct((1, 4), F32), in_sp...  51.1 us
    unnamed x1, local copies, waits for them, and re-layouts  1.19 us

profile of v5, /device:TPU:24, one launch (start us, length us, event | category | flops | bytes accessed | tf_op | source)
XLA Modules:
  0.0 53.6 jit_solution(1546252963140933129)
XLA Ops:
  1.3 51.1 %score_pairs.1 = f32[1,4]{1,0:T(1,128)} custom-call(bf16[9,32,256]{2,1,0:T(8,128)(2,1)} %bitcast.16, bf16[9,512,256]{2,1,0:T(8,128)(2,1)} %bitcast.14, s32[4,128]{1,0:T(4,128)} %bitcast.18, s32[4,128]{1,0:T(4,128)} %bitcast.19, s32[1]{0:T(128)S(6)} %copy.15.refs_4_, s32[512]{0:T(512)} %refs_5_.1, f32[9,1,32]{2,1,0:T(1,128)} %bitcast.20, f32[1,32]{1,0:T(1,128)} %bitcast.21, ...), custom_call_target="tpu_custom_call" | custom-call | tf_op jit(solution)/shard_map/score_pairs/pallas_call | solution.py:527
  52.5 1.2 %copy.17 = f32[1,4]{1,0:T(1,128)} copy(f32[1,4]{1,0:T(1,128)} %score_pairs.1) | data formatting | bytes 32
